TPU v7x, 256 devices: a whole 4x4x8 slice. The times are simulated.
256 devices in a mesh: rows: 16 (over z_lo, y, core), tm: 16 (over x, z_hi).
Axes of the slice: x: 4, y: 4, z: 8 (z_hi: 4, z_lo: 2; z = z_hi * 2 + z_lo), core: 2. Of those that a mesh axis runs over, the one named last changes fastest.
Arguments:
- residual: float32 [64, 1024, 512], P('tm', 'rows'), may hold values from -45 to 45
- cycle_weight: float32 [64, 1024, 512], P('tm', 'rows'), may hold values from -0.75 to 0.75
- cycle_offsets: int32 [64, 2], replicated, may hold values from -6 to 6, as said below
Outputs:
- new_weight: float32 [64, 1024, 512], P('tm', 'rows')
- error: float32 [64, 1024, 512], P('tm', 'rows')
Inputs may be any that keep to these rules, and one draw needn't show every extreme that they name: `cycle_offsets`: each row is a distinct (row, column) offset; together the rows are the 64 pixels (dy, dx) with 17 <= dy*dy + dx*dx <= 36, in an order drawn from the seed.
All inputs are finite; a program needn't handle non-finite values.
Results may differ from a plain program's by a relative error of at most 0.0003.
Values sent between devices are 32-bit elements; how exact they have to be, the bound alone decides.
A program may use at most 64 MiB of HBM per device.

v0:
```python
import jax
import jax.numpy as jnp
import numpy as np
from jax import lax
from jax.sharding import PartitionSpec as P


def with_halo(cells, sides, width):
    for axis, dim in sides:
        count = lax.axis_size(axis)
        ends = count - 1
        head = lax.slice_in_dim(cells, 0, width, axis=dim)
        tail = lax.slice_in_dim(cells, cells.shape[dim] - width, cells.shape[dim], axis=dim)
        cells = jnp.concatenate(
            [
                lax.ppermute(tail, axis, [(i, (i + 1) % count) for i in range(ends)]),
                cells,
                lax.ppermute(head, axis, [((i + 1) % count, i) for i in range(ends)]),
            ],
            axis=dim,
        )
    return cells


def cycle_points():
    points = []
    for row_off in range(-6, 7):
        for col_off in range(-6, 7):
            radius = row_off * row_off + col_off * col_off
            if radius >= 17 and radius <= 36:
                points.append((row_off, col_off))
    return points


def matching(cycle_offsets, points):
    table_rows = jnp.asarray(np.array([p[0] for p in points], dtype=np.int32))
    table_cols = jnp.asarray(np.array([p[1] for p in points], dtype=np.int32))
    same = (table_rows[:, None] == cycle_offsets[None, :, 0]) & (
        table_cols[:, None] == cycle_offsets[None, :, 1]
    )
    return same.astype(jnp.float32)


def reorder(selector, weights):
    return jnp.einsum("jk,kyx->jyx", selector, weights, precision=lax.Precision.HIGHEST)


def window_of(padded, point, height, width):
    return padded[:, 6 + point[0] : 6 + point[0] + height, 6 + point[1] : 6 + point[1] + width]


def cycle_passes(padded, centre, ordered_weight, points, height, width):
    background = jnp.zeros(centre.shape, jnp.float32)
    for index, point in enumerate(points):
        background = background + ordered_weight[index][None] * window_of(
            padded, point, height, width
        )
    error_part = centre - background
    grads = jnp.stack(
        [jnp.sum(error_part * window_of(padded, point, height, width), axis=0) for point in points]
    )
    squares = jnp.sum(padded * padded, axis=0)
    energy_sum = jnp.zeros((height, width), jnp.float32)
    for point in points:
        energy_sum = (
            energy_sum
            + squares[6 + point[0] : 6 + point[0] + height, 6 + point[1] : 6 + point[1] + width]
        )
    return (error_part, grads, energy_sum)


def on_device(residual, cycle_weight, cycle_offsets):
    frames_dev, rows_dev, cols = residual.shape
    cycle = cycle_offsets.shape[0]
    tm_count = lax.axis_size("tm")
    frames_all = frames_dev * tm_count
    points = cycle_points()
    selector = matching(cycle_offsets, points)
    extended = with_halo(residual, (("rows", 1),), 6)
    padded = jnp.pad(extended, ((0, 0), (0, 0), (6, 6)))
    columns = selector
    ordered_weight = reorder(columns, lax.all_gather(cycle_weight, "tm", axis=0, tiled=True))
    error, ordered_grad, local_energy = cycle_passes(
        padded, residual, ordered_weight, points, rows_dev, cols
    )
    columns = selector
    gradient = lax.psum_scatter(
        jnp.einsum("jk,jyx->kyx", columns, ordered_grad, precision=lax.Precision.HIGHEST),
        "tm",
        scatter_dimension=0,
        tiled=True,
    )
    energy = lax.psum(local_energy, "tm") / (cycle * frames_all) + 1e-06
    new_weight = cycle_weight + gradient / (frames_all * energy)[None]
    return (new_weight, error)


def solution(mesh):
    in_specs = (P("tm", "rows", None), P("tm", "rows", None), P())
    out_specs = (P("tm", "rows", None), P("tm", "rows", None))
    return jax.shard_map(
        on_device, mesh=mesh, in_specs=in_specs, out_specs=out_specs, check_vma=False
    )
```

profile of v0, /device:TPU:4, one launch (start us, length us, event | category | flops | bytes accessed | tf_op | source)
XLA Modules:
  0.0 429.7 jit_solution(9261241765014633690)
XLA Ops:
  8.0 0.9 fusion.19
  8.9 1.7 collective-permute-start
  10.6 1.3 collective-permute-start.1
  11.9 0.8 slice_bitcast_fusion.1
  12.7 1.1 constant_dynamic-update-slice_fusion.1
  13.8 1.4 collective-permute-done.1
  15.1 1.4 multiply_reduce_fusion
  16.5 2.8 slice_add_fusion
  19.9 97.1 %all-gather.2.cloned.1.call-done = f32[64,64,512]{2,1,0:T(8,128)} async-done(((f32[4,64,512]{2,1,0:T(8,128)}), f32[64,64,512]{2,1,0:T(8,128)}) %all-gather.2.cloned.1.call-update) | async-done | bytes 8388624 | tf_op jit(solution)/shard_map/all_gather | solution.py:82
  117.0 13.4 %fusion = f32[64,64,512]{2,0,1:T(8,128)S(1)} fusion(f32[64,64,512]{2,1,0:T(8,128)} %all-gather.2.cloned.1.call-done, s32[64]{0:T(128)S(1)} %copy-done.4, s32[64]{0:T(128)S(1)} %copy-done.3, s32[64]{0:T(128)S(1)} %get-tuple-element.146, s32[64]{0:T(128)S(1)} %get-tuple-element.145), kind=kOutput, calls=%fused_computation | convolution fusion | flops 1610625024 | bytes 16778240 | tf_op jit(solution)/shard_map/jk,kyx->jyx/dot_general | solution.py:45
  130.5 2.0 fusion.17
  132.4 2.3 fusion.15
  134.7 2.4 fusion.16
  138.8 9.4 %multiply_reduce_fusion.2 = (f32[64,512]{1,0:T(8,128)S(1)}, f32[64,512]{1,0:T(8,128)S(1)}, f32[64,512]{1,0:T(8,128)S(1)}, f32[64,512]{1,0:T(8,128)S(1)}, f32[64,...) fusion(f32[4,76,524]{2,1,0:T(8,128)S(1)} %get-tuple-element.142, ...), kind=kLoop, calls=%fused_computation.14 | loop fusion | flops 21168128 | bytes 44351488 | tf_op jit(solution)/shard_map/reduce_sum | solution.py:60
  148.3 2.5 multiply_reduce_fusion.39
  150.8 2.4 multiply_reduce_fusion.21
  154.3 0.7 stack.214
  155.0 0.7 stack.215
  156.5 0.7 stack.217
  157.9 0.7 stack.219
  158.7 0.7 stack.220
  159.4 0.7 stack.221
  161.6 0.7 stack.224
  163.1 0.7 stack.226
  163.9 0.7 stack.227
  164.6 0.7 stack.228
  166.1 0.7 stack.230
  166.8 0.7 stack.231
  167.6 0.7 stack.232
  168.3 0.7 stack.233
  169.1 0.7 stack.234
  171.3 0.7 stack.237
  172.0 0.7 stack.238
  172.7 0.9 multiply_reduce_fusion.1
  178.7 0.8 stack.248
  179.4 0.7 stack.249
  181.7 0.7 stack.252
  182.4 0.7 stack.253
  183.1 1.0 stack.255
  184.1 0.7 stack.256
  184.8 0.7 stack.257
  185.6 28.8 %stack.259 = f32[64,64,512]{2,0,1:T(8,128)} concatenate(f32[1,64,512]{2,0,1:T(1,128)S(1)} %stack.195, f32[1,64,512]{2,0,1:T(1,128)S(1)} %stack.196, f32[1,64,512]{2,0,1:T(1,128)S(1)} %stack.197, f32[1,64,512]{2,0,1:T(1,128)S(1)} %stack.198, f32[1,64,512]{2,0,1:T(1,128)S(1)} %stack.199, f32[1,64,512]{2,0,1:T(1,128)S(1)} %stack.200, f32[1,64,512]{2,0,1:T(1,128)S(1)} %stack.201, ...), dimensions={0} | concatenate | bytes 16777216 | tf_op jit(solution)/shard_map/stack | solution.py:59
  214.3 8.2 %fusion.5 = f32[64,64,512]{2,0,1:T(8,128)S(1)} fusion(f32[64,64,512]{2,0,1:T(8,128)} %stack.259, s32[64]{0:T(128)S(1)} %copy-done.4, s32[64]{0:T(128)S(1)} %copy-done.3, s32[64]{0:T(128)S(1)} %get-tuple-element.146, s32[64]{0:T(128)S(1)} %get-tuple-element.145), kind=kOutput, calls=%fused_computation.207 | convolution fusion | flops 1610625024 | bytes 16778240 | tf_op jit(solution)/shard_map/jk,jyx->kyx/dot_general | solution.py:88
  222.5 8.1 %copy.13 = f32[64,64,512]{2,1,0:T(8,128)} copy(f32[64,64,512]{2,0,1:T(8,128)S(1)} %fusion.5) | data formatting | bytes 16777216 | tf_op jit(solution)/shard_map/jk,jyx->kyx/dot_general | solution.py:88
  230.6 62.9 %all-reduce.3.cloned.1.call-done = f32[64,512]{1,0:T(8,128)} async-done(((f32[64,512]{1,0:T(8,128)}), f32[64,512]{1,0:T(8,128)}) %all-reduce.3.cloned.1.call-update) | async-done | bytes 131088 | tf_op jit(solution)/shard_map/psum | solution.py:93
  293.5 0.9 add_multiply_fusion
  294.4 126.6 %reduce-scatter.2.cloned.1.call-done = f32[4,64,512]{2,1,0:T(8,128)} async-done(((f32[64,64,512]{2,1,0:T(8,128)}), f32[4,64,512]{2,1,0:T(8,128)}) %reduce-scatter.2.cloned.1.call-update) | async-done | bytes 524304 | tf_op jit(solution)/shard_map/reduce_scatter | solution.py:87
  421.0 1.9 divide_add_fusion
  (91 shorter events, 16.0 us)
Async XLA Ops:
  7.2 109.9 %copy-start.3 = (s32[64]{0:T(128)S(1)}, s32[64]{0:T(128)}, u32[]{:S(2)}) copy-start(s32[64]{0:T(128)} %constant.15.clone) | copy-start | bytes 772
  7.2 109.9 %copy-start.4 = (s32[64]{0:T(128)S(1)}, s32[64]{0:T(128)}, u32[]{:S(2)}) copy-start(s32[64]{0:T(128)} %constant.16.clone) | copy-start | bytes 772
  7.2 109.8 %all-gather.2.cloned.1.call-start = ((), (), s32[]{:S(2)}) async-start(), calls=%async_computation.1 | async-start | bytes 8912896 | tf_op jit(solution)/shard_map/all_gather | solution.py:82
  7.9 285.6 %all-reduce.3.cloned.1.call-start = ((), (), s32[]{:S(2)}) async-start(), calls=%async_computation.3 | async-start | bytes 262144 | tf_op jit(solution)/shard_map/psum | solution.py:93
  8.9 4.9 %collective-permute-start = (f32[4,6,512]{2,1,0:T(8,128)S(1)}, f32[4,6,512]{2,1,0:T(8,128)S(1)}, u32[]{:S(2)}, u32[]{:S(2)}) collective-permute-start(f32[4,6,512]{2,1,0:T(8,128)S(1)} %get-tuple-element.143), channel_id=1, source_target_pairs={{0,16},{16,32},{32,48},{48,64},{64,80},{80,96},{96,112},{112,128},... | collective-permute-start | bytes 147464 | tf_op jit(solution)/shard_map/ppermute | solution.py:16
  10.6 4.5 %collective-permute-start.1 = (f32[4,6,512]{2,1,0:T(8,128)S(1)}, f32[4,6,512]{2,1,0:T(8,128)S(1)}, u32[]{:S(2)}, u32[]{:S(2)}) collective-permute-start(f32[4,6,512]{2,1,0:T(8,128)S(1)} %get-tuple-element.144), channel_id=1, source_target_pairs={{16,0},{32,16},{48,32},{64,48},{80,64},{96,80},{112,96},{128,112},... | collective-permute-start | bytes 147464 | tf_op jit(solution)/shard_map/ppermute | solution.py:18
  19.4 401.6 %reduce-scatter.2.cloned.1.call-start = ((), (), s32[]{:S(2)}) async-start(), calls=%async_computation.2 | async-start | bytes 8912896 | tf_op jit(solution)/shard_map/reduce_scatter | solution.py:87
  137.8 1.0 copy-start
  148.3 24.5 %copy-start.1 = (f32[4,64,512]{2,1,0:T(8,128)}, f32[4,64,512]{2,1,0:T(8,128)S(1)}, u32[]{:S(2)}) copy-start(f32[4,64,512]{2,1,0:T(8,128)S(1)} %get-tuple-element.76) | copy-start | bytes 1572868
  230.6 190.4 %copy-start.2 = (f32[4,64,512]{2,1,0:T(8,128)S(1)}, f32[4,64,512]{2,1,0:T(8,128)}, u32[]{:S(2)}) copy-start(f32[4,64,512]{2,1,0:T(8,128)} %param.6) | copy-start | bytes 1572868
Sparse Core Ops, SparseCore 0:
  10.4 106.5 all-gather.1
  119.6 173.7 all-reduce.2
  297.2 123.7 reduce-scatter.1
where the time goes:
time: 434 us; the launch traced here: 430 us
  waiting for transfers between devices  289 us (67%)
  local copies, waits for them, and re-layouts  79 us (18%)
  other arithmetic  22.3 us (5%)
  matrix products  21.6 us (5%)
  between operations  14.6 us (3%)
    reduce_scatter x1, waiting for transfers between devices, on_device(): lax.psum_scatter(jnp.einsum('jk,jyx->kyx', columns, ordered_grad, precisi...  127 us
    all_gather x1, waiting for transfers between devices, on_device(): lax.all_gather(cycle_weight, 'tm', axis=0, tiled=True)  97.1 us
    psum x1, waiting for transfers between devices, on_device(): energy = lax.psum(local_energy, 'tm') / (cycle * frames_all) + 1e-06  62.9 us
    another operation x65, local copies, waits for them, and re-layouts, cycle_passes(): jnp.stack([jnp.sum(error_part * window_of(padded, point, height, width),...  60.1 us
    reduce_sum x4, other arithmetic, cycle_passes(): jnp.sum(error_part * window_of(padded, point, height, width), axis=0)  15.2 us
    dot_general x1, matrix products, reorder(): jnp.einsum('jk,kyx->jyx', selector, weights, precision=lax.Precision.HIGH...  13.4 us
  transfers between devices with their start and end apart: 5, of which 4 were waited for; matrix products, arithmetic and copies ran while one was open for 28% of the time, Pallas kernels for 0%

commit v1 on v0

--- a/solution.py
+++ b/solution.py
@@ -79,7 +79,15 @@
     extended = with_halo(residual, (("rows", 1),), 6)
     padded = jnp.pad(extended, ((0, 0), (0, 0), (6, 6)))
     columns = selector
-    ordered_weight = reorder(columns, lax.all_gather(cycle_weight, "tm", axis=0, tiled=True))
+    ordered_weight = reorder(
+        columns,
+        jnp.concatenate(
+            lax.all_to_all(
+                jnp.stack([cycle_weight for _ in range(lax.axis_size("tm"))], 0), "tm", 0, 0
+            ),
+            0,
+        ),
+    )
     error, ordered_grad, local_energy = cycle_passes(
         padded, residual, ordered_weight, points, rows_dev, cols
     )

time: 434 us -> 536 us (1.24)
  waiting for transfers between devices: 289 us -> 360 us
  local copies, waits for them, and re-layouts: 79 us -> 103 us
  starting transfers between devices: 3.62 us -> 14.7 us
  matrix products: 21.6 us -> 16.1 us
    all_to_all x0 -> x1, waiting for transfers between devices: none -> 176 us  [on_device(): lax.all_to_all(jnp.stack([cycle_weight for _ in range(lax.axis_size('tm')...]
    all_gather x1 -> x0, waiting for transfers between devices: 97.1 us -> none  [on_device(): lax.all_gather(cycle_weight, 'tm', axis=0, tiled=True)]
    all_to_all x0 -> x1, starting transfers between devices: none -> 11.6 us  [on_device(): lax.all_to_all(jnp.stack([cycle_weight for _ in range(lax.axis_size('tm')...]
    reshape x0 -> x1, local copies, waits for them, and re-layouts: none -> 10 us  [on_device(): jnp.concatenate(lax.all_to_all(jnp.stack([cycle_weight for _ in range(lax...]
    all_to_all x0 -> x1, local copies, waits for them, and re-layouts: none -> 9.2 us  [on_device(): lax.all_to_all(jnp.stack([cycle_weight for _ in range(lax.axis_size('tm')...]
    psum x1, waiting for transfers between devices: 62.9 us -> 54 us  [on_device(): energy = lax.psum(local_energy, 'tm') / (cycle * frames_all) + 1e-06]
    dot_general x1, matrix products: 13.4 us -> 7.95 us  [reorder(): jnp.einsum('jk,kyx->jyx', selector, weights, precision=lax.Precision.HIGH...]
  transfers between devices with their start and end apart: 5 -> 5, of which waited for: 4 -> 4; matrix products, arithmetic and copies ran while one was open for 28% -> 25% of each run, Pallas kernels for 0% -> 0%
where the time goes in v1:
time: 536 us; the launch traced here: 530 us
  waiting for transfers between devices  360 us (67%)
  local copies, waits for them, and re-layouts  103 us (19%)
  other arithmetic  21.4 us (4%)
  matrix products  16.1 us (3%)
  between operations  14.9 us (3%)
  starting transfers between devices  14.7 us (3%)
    all_to_all x1, waiting for transfers between devices, on_device(): lax.all_to_all(jnp.stack([cycle_weight for _ in range(lax.axis_size('tm')...  176 us
    reduce_scatter x1, waiting for transfers between devices, on_device(): lax.psum_scatter(jnp.einsum('jk,jyx->kyx', columns, ordered_grad, precisi...  127 us
    another operation x65, local copies, waits for them, and re-layouts, cycle_passes(): jnp.stack([jnp.sum(error_part * window_of(padded, point, height, width),...  60.4 us
    psum x1, waiting for transfers between devices, on_device(): energy = lax.psum(local_energy, 'tm') / (cycle * frames_all) + 1e-06  54 us
    reduce_sum x4, other arithmetic, cycle_passes(): jnp.sum(error_part * window_of(padded, point, height, width), axis=0)  15.3 us
    all_to_all x1, starting transfers between devices, on_device(): lax.all_to_all(jnp.stack([cycle_weight for _ in range(lax.axis_size('tm')...  11.6 us
  transfers between devices with their start and end apart: 5, of which 4 were waited for; matrix products, arithmetic and copies ran while one was open for 25% of the time, Pallas kernels for 0%

profile of v1, /device:TPU:4, one launch (start us, length us, event | category | flops | bytes accessed | tf_op | source)
XLA Modules:
  0.0 530.1 jit_solution(7993910399045011845)
XLA Ops:
  7.2 1.4 copy.11
  8.5 4.8 stack.214
  13.4 11.6 %all-to-all-start = ((f32[16,4,64,512]{3,1,2,0:T(4,128)}), f32[16,4,64,512]{3,1,2,0:T(4,128)}, u32[]{:S(2)}, u32[]{:S(2)}) async-start(f32[16,4,64,512]{3,1,2,0:T(4,128)} %stack.214), calls=%async_computation | async-start | bytes 16777216 | tf_op jit(solution)/shard_map/all_to_all | solution.py:85
  25.0 1.3 collective-permute-start
  26.3 1.3 collective-permute-start.1
  27.7 3.6 collective-permute-done.1
  31.6 2.9 slice_add_fusion
  35.0 175.8 %all-to-all-done = f32[16,4,64,512]{3,1,2,0:T(4,128)} async-done(((f32[16,4,64,512]{3,1,2,0:T(4,128)}), f32[16,4,64,512]{3,1,2,0:T(4,128)}, u32[]{:S(2)}, u32[]{:S(2)}) %all-to-all-start) | async-done | bytes 8388640 | tf_op jit(solution)/shard_map/all_to_all | solution.py:85
  210.9 9.2 %copy.12 = f32[16,4,64,512]{3,1,0,2:T(4,128)} copy(f32[16,4,64,512]{3,1,2,0:T(4,128)} %all-to-all-done) | data formatting | bytes 16777216 | tf_op jit(solution)/shard_map/all_to_all | solution.py:85
  220.1 10.0 %reshape.14 = f32[64,64,512]{2,0,1:T(8,128)} reshape(f32[16,4,64,512]{3,1,0,2:T(4,128)} %copy.12) | data formatting | bytes 16777216 | tf_op jit(solution)/shard_map/reshape | solution.py:84
  230.1 7.9 %fusion.2 = f32[64,64,512]{2,0,1:T(8,128)S(1)} fusion(f32[64,64,512]{2,0,1:T(8,128)} %reshape.14, s32[64]{0:T(128)S(1)} %copy-done.4, s32[64]{0:T(128)S(1)} %copy-done.3, s32[64]{0:T(128)S(1)} %get-tuple-element.146, s32[64]{0:T(128)S(1)} %get-tuple-element.145), kind=kOutput, calls=%fused_computation.204 | convolution fusion | flops 1610625024 | bytes 16778240 | tf_op jit(solution)/shard_map/jk,kyx->jyx/dot_general | solution.py:45
  238.1 2.3 fusion.14
  240.4 2.5 fusion.15
  242.9 2.5 fusion.16
  246.9 9.6 %multiply_reduce_fusion.2 = (f32[64,512]{1,0:T(8,128)S(1)}, f32[64,512]{1,0:T(8,128)S(1)}, f32[64,512]{1,0:T(8,128)S(1)}, f32[64,512]{1,0:T(8,128)S(1)}, f32[64,...) fusion(f32[4,76,524]{2,1,0:T(8,128)S(1)} %get-tuple-element.142, ...), kind=kLoop, calls=%fused_computation.12 | loop fusion | flops 21168128 | bytes 44351488 | tf_op jit(solution)/shard_map/reduce_sum | solution.py:60
  256.5 2.5 multiply_reduce_fusion.39
  259.0 2.4 multiply_reduce_fusion.21
  262.1 0.7 stack.230
  262.9 0.7 stack.231
  264.3 0.7 stack.233
  265.8 0.7 stack.235
  266.5 0.7 stack.236
  267.3 0.7 stack.237
  268.0 0.7 stack.238
  268.8 0.7 stack.239
  271.0 0.7 stack.242
  272.5 0.7 stack.244
  273.2 0.7 stack.245
  273.9 0.7 stack.246
  275.4 0.7 stack.248
  276.2 0.7 stack.249
  276.9 0.7 stack.250
  277.6 0.7 stack.251
  278.4 0.7 stack.252
  281.3 0.7 stack.256
  283.5 0.9 multiply_reduce_fusion.1
  288.5 0.8 stack.271
  289.3 0.7 stack.272
  290.8 0.9 stack.275
  291.7 0.7 stack.276
  292.4 0.7 stack.277
  293.2 29.8 %stack.279 = f32[64,64,512]{2,0,1:T(8,128)} concatenate(f32[1,64,512]{2,0,1:T(1,128)S(1)} %stack.215, f32[1,64,512]{2,0,1:T(1,128)S(1)} %stack.216, f32[1,64,512]{2,0,1:T(1,128)S(1)} %stack.217, f32[1,64,512]{2,0,1:T(1,128)S(1)} %stack.218, f32[1,64,512]{2,0,1:T(1,128)S(1)} %stack.219, f32[1,64,512]{2,0,1:T(1,128)S(1)} %stack.220, f32[1,64,512]{2,0,1:T(1,128)S(1)} %stack.221, ...), dimensions={0} | concatenate | bytes 16777216 | tf_op jit(solution)/shard_map/stack | solution.py:59
  322.9 8.2 %fusion.4 = f32[64,64,512]{2,0,1:T(8,128)S(1)} fusion(f32[64,64,512]{2,0,1:T(8,128)} %stack.279, s32[64]{0:T(128)S(1)} %copy-done.4, s32[64]{0:T(128)S(1)} %copy-done.3, s32[64]{0:T(128)S(1)} %get-tuple-element.146, s32[64]{0:T(128)S(1)} %get-tuple-element.145), kind=kOutput, calls=%fused_computation.206 | convolution fusion | flops 1610625024 | bytes 16778240 | tf_op jit(solution)/shard_map/jk,jyx->kyx/dot_general | solution.py:96
  331.1 8.1 %copy.14 = f32[64,64,512]{2,1,0:T(8,128)} copy(f32[64,64,512]{2,0,1:T(8,128)S(1)} %fusion.4) | data formatting | bytes 16777216 | tf_op jit(solution)/shard_map/jk,jyx->kyx/dot_general | solution.py:96
  339.2 54.0 %all-reduce.3.cloned.1.call-done = f32[64,512]{1,0:T(8,128)} async-done(((f32[64,512]{1,0:T(8,128)}), f32[64,512]{1,0:T(8,128)}) %all-reduce.3.cloned.1.call-update) | async-done | bytes 131088 | tf_op jit(solution)/shard_map/psum | solution.py:101
  393.2 0.9 add_multiply_fusion
  394.1 127.0 %reduce-scatter.2.cloned.1.call-done = f32[4,64,512]{2,1,0:T(8,128)} async-done(((f32[64,64,512]{2,1,0:T(8,128)}), f32[4,64,512]{2,1,0:T(8,128)}) %reduce-scatter.2.cloned.1.call-update) | async-done | bytes 524304 | tf_op jit(solution)/shard_map/reduce_scatter | solution.py:95
  521.1 1.9 divide_add_fusion
  (96 shorter events, 15.6 us)
Async XLA Ops:
  13.4 11.6 %copy-start = (f32[4,64,512]{2,1,0:T(8,128)S(1)}, f32[4,64,512]{2,1,0:T(8,128)}, u32[]{:S(2)}) copy-start(f32[4,64,512]{2,1,0:T(8,128)} %param.5) | copy-start | bytes 1572868
  13.4 14.3 %copy-start.5 = (s32[64,2]{0,1:T(2,128)S(1)}, s32[64,2]{0,1:T(2,128)}, u32[]{:S(2)}) copy-start(s32[64,2]{0,1:T(2,128)} %param.7) | copy-start | bytes 1540
  13.4 197.5 %all-to-all-start = ((f32[16,4,64,512]{3,1,2,0:T(4,128)}), f32[16,4,64,512]{3,1,2,0:T(4,128)}, u32[]{:S(2)}, u32[]{:S(2)}) async-start(f32[16,4,64,512]{3,1,2,0:T(4,128)} %stack.214), calls=%async_computation | async-start | bytes 16777216 | tf_op jit(solution)/shard_map/all_to_all | solution.py:85
  25.0 368.2 %all-reduce.3.cloned.1.call-start = ((), (), s32[]{:S(2)}) async-start(), calls=%async_computation.3 | async-start | bytes 262144 | tf_op jit(solution)/shard_map/psum | solution.py:101
  25.0 2.7 collective-permute-start
  26.3 5.0 collective-permute-start.1
  34.5 486.6 %reduce-scatter.2.cloned.1.call-start = ((), (), s32[]{:S(2)}) async-start(), calls=%async_computation.2 | async-start | bytes 8912896 | tf_op jit(solution)/shard_map/reduce_scatter | solution.py:95
  220.1 10.0 %copy-start.3 = (s32[64]{0:T(128)S(1)}, s32[64]{0:T(128)}, u32[]{:S(2)}) copy-start(s32[64]{0:T(128)} %constant.15.clone) | copy-start | bytes 772
  220.1 10.0 %copy-start.4 = (s32[64]{0:T(128)S(1)}, s32[64]{0:T(128)}, u32[]{:S(2)}) copy-start(s32[64]{0:T(128)} %constant.16.clone) | copy-start | bytes 772
  256.5 27.0 %copy-start.1 = (f32[4,64,512]{2,1,0:T(8,128)}, f32[4,64,512]{2,1,0:T(8,128)S(1)}, u32[]{:S(2)}) copy-start(f32[4,64,512]{2,1,0:T(8,128)S(1)} %get-tuple-element.76) | copy-start | bytes 1572868
  339.2 181.9 %copy-start.2 = (f32[4,64,512]{2,1,0:T(8,128)S(1)}, f32[4,64,512]{2,1,0:T(8,128)}, u32[]{:S(2)}) copy-start(f32[4,64,512]{2,1,0:T(8,128)} %param.6) | copy-start | bytes 1572868
Sparse Core Ops, SparseCore 0:
  34.6 358.4 all-reduce.2
  396.9 124.1 reduce-scatter.1
